TPU v7x, 128 devices: a whole 4x4x4 slice. The times are simulated.
128 devices in a mesh: row: 4 (over z), col: 16 (over x, y), gz: 2 (over core).
Axes of the slice: x: 4, y: 4, z: 4, core: 2. Of those that a mesh axis runs over, the one named last changes fastest.
Arguments:
- rhs_half: float32 [2, 3, 64, 4096], P('gz', None, None, ('row', 'col')), may hold values from -6 to 6
- rhs_root: float32 [64, 4096], P(None, ('row', 'col')), may hold values from -6 to 6
- lower_coupling: bfloat16 [2, 5, 4096, 4096], P('gz', None, 'col', 'row'), may hold values from -0.046875 to 0.046875
- lower_pattern: int32 [2, 5, 32, 32], P('gz', None, 'col', 'row'), may hold values 0 or 1
- upper_coupling: bfloat16 [2, 5, 4096, 4096], P('gz', None, 'col', 'row'), may hold values from -0.046875 to 0.046875
- upper_pattern: int32 [2, 5, 32, 32], P('gz', None, 'col', 'row'), may hold values 0 or 1
- lower_inverse: bfloat16 [2, 3, 4096, 4096], P('gz', None, 'col', 'row'), may hold values from -0.09375 to 0.09375
- upper_inverse: bfloat16 [2, 3, 4096, 4096], P('gz', None, 'col', 'row'), may hold values from -0.09375 to 0.09375
- root_lower_inverse: bfloat16 [4096, 4096], P('col', 'row'), may hold values from -0.09375 to 0.09375
- root_upper_inverse: bfloat16 [4096, 4096], P('col', 'row'), may hold values from -0.09375 to 0.09375
Outputs:
- sol_half: float32 [2, 3, 64, 4096], P('gz', None, None, ('row', 'col'))
- sol_root: float32 [64, 4096], P(None, ('row', 'col'))
All inputs are finite; a program needn't handle non-finite values. No bound on the sum of `lower_pattern` or of `upper_pattern` on one device may be relied on, other than what follows from the above.
Results may differ from a plain program's by a relative error of at most 0.007.
Values may be sent and summed in bfloat16 or wider, within the bound.
A program may use at most 64 MiB of HBM per device.

v0:
```python
import jax
import jax.numpy as jnp
from jax import lax
from jax.sharding import PartitionSpec as P


def apply_mask(tiles, pattern):
    count, across, down = pattern.shape
    shaped = tiles.reshape(count, across, tiles.shape[1] // across, down, tiles.shape[2] // down)
    shaped = shaped * pattern[:, :, None, :, None].astype(jnp.bfloat16)
    return shaped.reshape(tiles.shape)


def multiply(vectors, tiles):
    return jnp.einsum("snj,sji->sni", vectors, tiles, preferred_element_type=jnp.float32)


def multiply_one(vectors, tiles):
    return jnp.einsum("nj,sji->sni", vectors[0], tiles, preferred_element_type=jnp.float32)


def settle(partial_value, offset_bias, column, narrow):
    share_width = offset_bias.shape[2]
    slot = (
        lax.dynamic_slice_in_dim(partial_value, column * share_width, share_width, 2) + offset_bias
    )
    partial_value = lax.dynamic_update_slice_in_dim(partial_value, slot, column * share_width, 2)
    summed = lax.psum(partial_value, "col")
    owned = lax.dynamic_slice_in_dim(summed, column * share_width, share_width, 2)
    gathered = lax.all_gather(summed.astype(jnp.bfloat16), "row", axis=2, tiled=True)
    return (owned, lax.dynamic_slice_in_dim(gathered, column * narrow, narrow, 2))


def per_device(
    rhs_half,
    rhs_root,
    lower_coupling,
    lower_pattern,
    upper_coupling,
    upper_pattern,
    lower_inverse,
    upper_inverse,
    root_lower_inverse,
    root_upper_inverse,
):
    column = lax.axis_index("col")
    lower = apply_mask(lower_coupling[0], lower_pattern[0])
    upper = apply_mask(upper_coupling[0], upper_pattern[0])
    narrow = lower.shape[1]
    share_width = rhs_half.shape[3]
    nrhs_count = rhs_half.shape[2]

    def zeros_for(count):
        return jnp.zeros((count, nrhs_count, share_width), jnp.float32)

    leaf_full = lax.all_gather(
        rhs_half[0, 1:3].astype(jnp.bfloat16), ("row", "col"), axis=2, tiled=True
    )
    leaf_input = lax.dynamic_slice_in_dim(leaf_full, column * narrow, narrow, 2)
    leaf_value, leaf_cols = settle(
        multiply(leaf_input, lower_inverse[0, 1:3]), zeros_for(2), column, narrow
    )
    top_terms = -multiply(leaf_cols, lower[0:2]).sum(axis=0, keepdims=True)
    top_rest, top_input = settle(top_terms, rhs_half[0, 0:1], column, narrow)
    top_value, top_cols = settle(
        multiply(top_input, lower_inverse[0, 0:1]), zeros_for(1), column, narrow
    )
    every_cols = jnp.concatenate([top_cols, leaf_cols], axis=0)
    root_terms = -multiply(every_cols, lower[2:5]).sum(axis=0, keepdims=True)
    root_terms = lax.psum(root_terms, "gz")
    root_rest, root_input = settle(root_terms, rhs_root[None], column, narrow)
    root_value, root_cols = settle(
        multiply(root_input, root_lower_inverse[None]), zeros_for(1), column, narrow
    )
    root_back, root_back_cols = settle(
        multiply(root_cols, root_upper_inverse[None]), zeros_for(1), column, narrow
    )
    first_terms = -multiply_one(root_back_cols, upper[2:3])
    first_rest, first_input = settle(first_terms, top_value, column, narrow)
    first_back, first_back_cols = settle(
        multiply(first_input, upper_inverse[0, 0:1]), zeros_for(1), column, narrow
    )
    second_terms = -(
        multiply_one(root_back_cols, upper[3:5]) + multiply_one(first_back_cols, upper[0:2])
    )
    second_rest, second_input = settle(second_terms, leaf_value, column, narrow)
    second_back, second_back_cols = settle(
        multiply(second_input, upper_inverse[0, 1:3]), zeros_for(2), column, narrow
    )
    sol_half = jnp.concatenate([first_back, second_back], axis=0)[None]
    return (sol_half, root_back[0])


def solution(mesh):
    in_specs = (
        P("gz", None, None, ("row", "col")),
        P(None, ("row", "col")),
        P("gz", None, "col", "row"),
        P("gz", None, "col", "row"),
        P("gz", None, "col", "row"),
        P("gz", None, "col", "row"),
        P("gz", None, "col", "row"),
        P("gz", None, "col", "row"),
        P("col", "row"),
        P("col", "row"),
    )
    out_specs = (P("gz", None, None, ("row", "col")), P(None, ("row", "col")))
    return jax.shard_map(
        per_device, mesh=mesh, in_specs=in_specs, out_specs=out_specs, check_vma=False
    )
```

profile of v0, /device:TPU:0, one launch (start us, length us, event | category | flops | bytes accessed | tf_op | source)
XLA Modules:
  0.0 1071.1 jit_solution(17997548227670011957)
XLA Ops:
  7.2 1.0 slice.86
  9.0 70.3 %all-gather.9.cloned.1.call-done = bf16[1,2,64,4096]{2,1,0,3:T(2,128)(2,1)} async-done(((bf16[1,2,64,64]{2,1,0,3:T(2,128)(2,1)}), bf16[1,2,64,4096]{2,1,0,3:T(2,128)(2,1)}) %all-gather.9.cloned.1.call-update) | async-done | bytes 1048592 | tf_op jit(solution)/shard_map/all_gather | solution.py:56
  79.3 1.0 constant_dynamic-slice_fusion.6
  80.4 1.5 fusion.6
  82.9 1.6 dynamic_update_slice.30
  84.5 83.1 %all-reduce.12.cloned.1.call-done = f32[2,64,1024]{2,1,0:T(8,128)} async-done(((f32[2,64,1024]{2,1,0:T(8,128)}), f32[2,64,1024]{2,1,0:T(8,128)}) %all-reduce.12.cloned.1.call-update) | async-done | bytes 524304 | tf_op jit(solution)/shard_map/psum | solution.py:28
  167.6 1.8 convert_element_type.56
  170.4 1.0 slice.63
  171.4 2.3 slice.51
  173.7 19.6 %all-gather.5.cloned.1.call-done = bf16[2,64,4096]{2,1,0:T(8,128)(2,1)} async-done(((bf16[2,64,1024]{2,1,0:T(8,128)(2,1)}), bf16[2,64,4096]{2,1,0:T(8,128)(2,1)}) %all-gather.5.cloned.1.call-update) | async-done | bytes 1048592 | tf_op jit(solution)/shard_map/all_gather | solution.py:30
  194.2 1.5 fusion.1
  197.0 77.2 %all-reduce.23 = bf16[1,64,1024]{2,1,0:T(8,128)(2,1)} all-reduce(f32[1,64,1024]{2,1,0:T(8,128)S(1)} %dynamic_update_slice.31), channel_id=1, replica_groups=mesh['row'=4,'col'=16,'gz'=2] {'col'}, use_global_device_ids=true, to_apply=%region_1.0 | all-reduce | flops 65536 | bytes 393216 | tf_op jit(solution)/shard_map/psum | solution.py:28
  274.2 13.0 %all_gather.32 = bf16[1,64,4096]{2,1,0:T(8,128)(2,1)S(1)} all-gather(bf16[1,64,1024]{2,1,0:T(8,128)(2,1)} %all-reduce.23), channel_id=1, replica_groups=mesh['row'=4,'col'=16,'gz'=2] {'row'}, dimensions={2}, use_global_device_ids=true | all-gather | bytes 655360 | tf_op jit(solution)/shard_map/all_gather | solution.py:30
  287.2 1.2 fusion.14
  289.7 1.3 slice.64
  291.0 2.5 slice.55
  293.5 3.9 copy.17
  297.4 72.5 %all-reduce.14.cloned.1.call-done = f32[1,64,1024]{2,1,0:T(8,128)} async-done(((f32[1,64,1024]{2,1,0:T(8,128)}), f32[1,64,1024]{2,1,0:T(8,128)}) %all-reduce.14.cloned.1.call-update) | async-done | bytes 262160 | tf_op jit(solution)/shard_map/psum | solution.py:28
  370.0 1.0 convert_element_type.60
  370.9 13.8 %all_gather.33 = bf16[1,64,4096]{2,1,0:T(8,128)(2,1)S(1)} all-gather(bf16[1,64,1024]{2,1,0:T(8,128)(2,1)S(1)} %convert_element_type.60), channel_id=1, replica_groups=mesh['row'=4,'col'=16,'gz'=2] {'row'}, dimensions={2}, use_global_device_ids=true | all-gather | bytes 655360 | tf_op jit(solution)/shard_map/all_gather | solution.py:30
  384.8 1.1 fusion.3
  386.0 2.0 broadcast_multiply_fusion.1
  388.0 20.1 %all-reduce.16.cloned.1.call-done = f32[1,64,1024]{2,1,0:T(8,128)} async-done(((f32[1,64,1024]{2,1,0:T(8,128)}), f32[1,64,1024]{2,1,0:T(8,128)}) %all-reduce.16.cloned.1.call-update) | async-done | bytes 262160 | tf_op jit(solution)/shard_map/psum | solution.py:70
  408.9 1.4 dynamic_update_slice.33
  410.4 77.5 %all-reduce.24 = bf16[1,64,1024]{2,1,0:T(8,128)(2,1)S(1)} all-reduce(f32[1,64,1024]{2,1,0:T(8,128)} %dynamic_update_slice.33), channel_id=1, replica_groups=mesh['row'=4,'col'=16,'gz'=2] {'col'}, use_global_device_ids=true, to_apply=%region_4.0 | all-reduce | flops 65536 | bytes 393216 | tf_op jit(solution)/shard_map/psum | solution.py:28
  487.9 13.3 %all_gather.34 = bf16[1,64,4096]{2,1,0:T(8,128)(2,1)S(1)} all-gather(bf16[1,64,1024]{2,1,0:T(8,128)(2,1)S(1)} %all-reduce.24), channel_id=1, replica_groups=mesh['row'=4,'col'=16,'gz'=2] {'row'}, dimensions={2}, use_global_device_ids=true | all-gather | bytes 655360 | tf_op jit(solution)/shard_map/all_gather | solution.py:30
  501.8 71.9 %all-reduce.25 = bf16[1,64,1024]{2,1,0:T(8,128)(2,1)S(1)} all-reduce(f32[1,64,1024]{2,1,0:T(8,128)S(1)} %dynamic_update_slice.34), channel_id=1, replica_groups=mesh['row'=4,'col'=16,'gz'=2] {'col'}, use_global_device_ids=true, to_apply=%region_5.0 | all-reduce | flops 65536 | bytes 393216 | tf_op jit(solution)/shard_map/psum | solution.py:28
  573.8 12.8 %all_gather.35 = bf16[1,64,4096]{2,1,0:T(8,128)(2,1)S(1)} all-gather(bf16[1,64,1024]{2,1,0:T(8,128)(2,1)S(1)} %all-reduce.25), channel_id=1, replica_groups=mesh['row'=4,'col'=16,'gz'=2] {'row'}, dimensions={2}, use_global_device_ids=true | all-gather | bytes 655360 | tf_op jit(solution)/shard_map/all_gather | solution.py:30
  586.6 1.3 fusion.28
  589.1 1.5 fusion.50
  590.6 1.5 slice.60
  592.1 1.6 slice.58
  593.7 77.1 %all-reduce.18.cloned.1.call-done = f32[1,64,1024]{2,1,0:T(8,128)} async-done(((f32[1,64,1024]{2,1,0:T(8,128)}), f32[1,64,1024]{2,1,0:T(8,128)}) %all-reduce.18.cloned.1.call-update) | async-done | bytes 262160 | tf_op jit(solution)/shard_map/psum | solution.py:28
  670.9 1.0 convert_element_type.63
  671.8 13.8 %all_gather.36 = bf16[1,64,4096]{2,1,0:T(8,128)(2,1)S(1)} all-gather(bf16[1,64,1024]{2,1,0:T(8,128)(2,1)S(1)} %convert_element_type.63), channel_id=1, replica_groups=mesh['row'=4,'col'=16,'gz'=2] {'row'}, dimensions={2}, use_global_device_ids=true | all-gather | bytes 655360 | tf_op jit(solution)/shard_map/all_gather | solution.py:30
  687.2 74.7 %all-reduce.26 = bf16[1,64,1024]{2,1,0:T(8,128)(2,1)S(1)} all-reduce(f32[1,64,1024]{2,1,0:T(8,128)S(1)} %dynamic_update_slice.36), channel_id=1, replica_groups=mesh['row'=4,'col'=16,'gz'=2] {'col'}, use_global_device_ids=true, to_apply=%region_7.0 | all-reduce | flops 65536 | bytes 393216 | tf_op jit(solution)/shard_map/psum | solution.py:28
  761.9 12.8 %all_gather.37 = bf16[1,64,4096]{2,1,0:T(8,128)(2,1)S(1)} all-gather(bf16[1,64,1024]{2,1,0:T(8,128)(2,1)S(1)} %all-reduce.26), channel_id=1, replica_groups=mesh['row'=4,'col'=16,'gz'=2] {'row'}, dimensions={2}, use_global_device_ids=true | all-gather | bytes 655360 | tf_op jit(solution)/shard_map/all_gather | solution.py:30
  774.7 1.3 fusion.12
  777.2 1.9 fusion.24
  779.1 78.6 %all-reduce.20.cloned.1.call-done = f32[1,64,1024]{2,1,0:T(8,128)} async-done(((f32[1,64,1024]{2,1,0:T(8,128)}), f32[1,64,1024]{2,1,0:T(8,128)}) %all-reduce.20.cloned.1.call-update) | async-done | bytes 262160 | tf_op jit(solution)/shard_map/psum | solution.py:28
  857.7 1.0 convert_element_type.65
  858.7 13.8 %all_gather.38 = bf16[1,64,4096]{2,1,0:T(8,128)(2,1)S(1)} all-gather(bf16[1,64,1024]{2,1,0:T(8,128)(2,1)S(1)} %convert_element_type.65), channel_id=1, replica_groups=mesh['row'=4,'col'=16,'gz'=2] {'row'}, dimensions={2}, use_global_device_ids=true | all-gather | bytes 655360 | tf_op jit(solution)/shard_map/all_gather | solution.py:30
  872.5 1.3 fusion
  875.3 78.4 %all-reduce.27 = bf16[2,64,1024]{2,1,0:T(8,128)(2,1)} all-reduce(f32[2,64,1024]{2,1,0:T(8,128)S(1)} %dynamic_update_slice.38), channel_id=1, replica_groups=mesh['row'=4,'col'=16,'gz'=2] {'col'}, use_global_device_ids=true, to_apply=%region_9.0 | all-reduce | flops 131072 | bytes 786432 | tf_op jit(solution)/shard_map/psum | solution.py:28
  953.7 20.4 %all-gather.7.cloned.1.call-done = bf16[2,64,4096]{2,1,0:T(8,128)(2,1)} async-done(((bf16[2,64,1024]{2,1,0:T(8,128)(2,1)}), bf16[2,64,4096]{2,1,0:T(8,128)(2,1)}) %all-gather.7.cloned.1.call-update) | async-done | bytes 1048592 | tf_op jit(solution)/shard_map/all_gather | solution.py:30
  974.1 1.6 fusion.4
  977.1 1.5 dynamic-slice_bitcast_fusion
  979.4 83.6 %all-reduce.22.cloned.1.call-done = f32[2,64,1024]{2,1,0:T(8,128)} async-done(((f32[2,64,1024]{2,1,0:T(8,128)}), f32[2,64,1024]{2,1,0:T(8,128)}) %all-reduce.22.cloned.1.call-update) | async-done | bytes 524304 | tf_op jit(solution)/shard_map/psum | solution.py:28
  (75 shorter events, 17.0 us)
Async XLA Ops:
  7.2 494.0 %copy-start = (bf16[256,1024]{1,0:T(8,128)(2,1)S(1)}, bf16[256,1024]{1,0:T(8,128)(2,1)}, u32[]{:S(2)}) copy-start(bf16[256,1024]{1,0:T(8,128)(2,1)} %param.18) | copy-start | bytes 1572868
  7.2 162.2 %copy-start.2 = (bf16[1,5,256,1024]{3,2,1,0:T(8,128)(2,1)S(1)}, bf16[1,5,256,1024]{3,2,1,0:T(8,128)(2,1)}, u32[]{:S(2)}) copy-start(bf16[1,5,256,1024]{3,2,1,0:T(8,128)(2,1)} %param.12) | copy-start | bytes 7864324
  7.2 72.2 %all-gather.9.cloned.1.call-start = ((), (), s32[]{:S(2)}) async-start(), calls=%async_computation.8 | async-start | bytes 2129920 | tf_op jit(solution)/shard_map/all_gather | solution.py:56
  9.0 158.6 %all-reduce.12.cloned.1.call-start = ((), (), s32[]{:S(2)}) async-start(), calls=%async_computation | async-start | bytes 1048576 | tf_op jit(solution)/shard_map/psum | solution.py:28
  82.0 0.8 copy-start.3
  84.4 108.9 %all-gather.5.cloned.1.call-start = ((), (), s32[]{:S(2)}) async-start(), calls=%async_computation.1 | async-start | bytes 1310720 | tf_op jit(solution)/shard_map/all_gather | solution.py:30
  169.4 200.6 %all-reduce.14.cloned.1.call-start = ((), (), s32[]{:S(2)}) async-start(), calls=%async_computation.2 | async-start | bytes 524288 | tf_op jit(solution)/shard_map/psum | solution.py:28
  169.4 0.7 copy-start.10
  288.9 0.7 copy-start.5
  289.6 118.4 %all-reduce.16.cloned.1.call-start = ((), (), s32[]{:S(2)}) async-start(), calls=%async_computation.3 | async-start | bytes 524288 | tf_op jit(solution)/shard_map/psum | solution.py:70
  293.5 3.9 copy-start.11
  385.9 285.0 %all-reduce.18.cloned.1.call-start = ((), (), s32[]{:S(2)}) async-start(), calls=%async_computation.4 | async-start | bytes 524288 | tf_op jit(solution)/shard_map/psum | solution.py:28
  386.0 22.1 %copy-start.9 = (f32[64,64]{1,0:T(8,128)S(1)}, f32[64,64]{1,0:T(8,128)}, u32[]{:S(2)}) copy-start(f32[64,64]{1,0:T(8,128)} %param.11) | copy-start | bytes 49156
  388.0 201.2 %copy-start.1 = (bf16[5,2,128,8,128]{4,3,2,1,0:T(8,128)(2,1)}, bf16[5,2,128,8,128]{4,3,2,1,0:T(8,128)(2,1)S(1)}, u32[]{:S(2)}) copy-start(bf16[5,2,128,8,128]{4,3,2,1,0:T(8,128)(2,1)S(1)} %broadcast_multiply_fusion.1) | copy-start | bytes 7864324
  588.3 0.7 copy-start.6
  589.1 268.7 %all-reduce.20.cloned.1.call-start = ((), (), s32[]{:S(2)}) async-start(), calls=%async_computation.5 | async-start | bytes 524288 | tf_op jit(solution)/shard_map/psum | solution.py:28
  592.1 93.5 %slice-start = ((bf16[5,2,128,8,128]{4,3,2,1,0:T(8,128)(2,1)}), bf16[1,2,128,8,128]{4,3,2,1,0:T(8,128)(2,1)S(1)}, s32[]{:S(2)}) async-start(bf16[5,2,128,8,128]{4,3,2,1,0:T(8,128)(2,1)} %copy-done.1), calls=%async_computation.9 | async-start | bytes 1048576 | tf_op jit(solution)/shard_map/slice | solution.py:78
  685.7 1.1 copy-start.8
  776.5 0.7 copy-start.7
  777.2 197.0 %all-gather.7.cloned.1.call-start = ((), (), s32[]{:S(2)}) async-start(), calls=%async_computation.6 | async-start | bytes 1310720 | tf_op jit(solution)/shard_map/all_gather | solution.py:30
  953.7 109.3 %all-reduce.22.cloned.1.call-start = ((), (), s32[]{:S(2)}) async-start(), calls=%async_computation.7 | async-start | bytes 1048576 | tf_op jit(solution)/shard_map/psum | solution.py:28
  976.3 0.8 copy-start.4
Sparse Core Ops, SparseCore 0:
  11.4 67.8 all-gather.8
  84.6 82.9 all-reduce.11
  169.5 23.8 all-gather.4
  289.8 80.1 all-reduce.13
  386.0 22.0 all-reduce.15
  589.2 81.6 all-reduce.17
  777.3 80.3 all-reduce.19
  953.8 20.2 all-gather.6
  977.3 85.5 all-reduce.21
where the time goes:
time: 1070 us
  waiting for transfers between devices  526 us (49%)
  blocking collectives  473 us (44%)
  local copies, waits for them, and re-layouts  33.8 us (3%)
  between operations  14.2 us (1%)
  matrix products  13.1 us (1%)
  other arithmetic  11 us (1%)
    psum x5, waiting for transfers between devices, settle(): summed = lax.psum(partial_value, 'col')  395 us
    psum x5, blocking collectives, settle(): summed = lax.psum(partial_value, 'col')  380 us
    all_gather x7, blocking collectives, settle(): lax.all_gather(summed.astype(jnp.bfloat16), 'row', axis=2, tiled=True)  93.3 us
    all_gather x1, waiting for transfers between devices, per_device(): lax.all_gather(rhs_half[0, 1:3].astype(jnp.bfloat16), ('row', 'col'), axi...  70.3 us
    all_gather x2, waiting for transfers between devices, settle(): lax.all_gather(summed.astype(jnp.bfloat16), 'row', axis=2, tiled=True)  40 us
  transfers between devices with their start and end apart: 9, of which 9 were waited for; matrix products, arithmetic and copies ran while one was open for 2% of the time, Pallas kernels for 0%

commit v1 on v0

--- a/solution.py
+++ b/solution.py
@@ -27,7 +27,16 @@
     partial_value = lax.dynamic_update_slice_in_dim(partial_value, slot, column * share_width, 2)
     summed = lax.psum(partial_value, "col")
     owned = lax.dynamic_slice_in_dim(summed, column * share_width, share_width, 2)
-    gathered = lax.all_gather(summed.astype(jnp.bfloat16), "row", axis=2, tiled=True)
+    unit = summed.astype(jnp.bfloat16)
+    gathered = jnp.concatenate(
+        lax.all_to_all(
+            jnp.stack([unit] * lax.psum(1, axis_name="row"), axis=0),
+            axis_name="row",
+            split_axis=0,
+            concat_axis=0,
+        ),
+        axis=2,
+    )
     return (owned, lax.dynamic_slice_in_dim(gathered, column * narrow, narrow, 2))
 
 

time: 1070 us -> 1040 us (0.972)
  blocking collectives: 473 us -> 434 us
  starting transfers between devices: 0.37 us -> 17.8 us
    all_gather x7 -> x0, blocking collectives: 93.3 us -> none  [settle(): lax.all_gather(summed.astype(jnp.bfloat16), 'row', axis=2, tiled=True)]
    all_to_all x0 -> x5, blocking collectives: none -> 57.2 us  [settle(): lax.all_to_all(jnp.stack([unit] * lax.psum(1, axis_name='row'), axis=0),...]
    all_gather x2 -> x0, waiting for transfers between devices: 40 us -> none  [settle(): lax.all_gather(summed.astype(jnp.bfloat16), 'row', axis=2, tiled=True)]
    all_to_all x0 -> x4, waiting for transfers between devices: none -> 22.3 us  [settle(): lax.all_to_all(jnp.stack([unit] * lax.psum(1, axis_name='row'), axis=0),...]
    all_to_all x0 -> x4, starting transfers between devices: none -> 17.7 us  [settle(): lax.all_to_all(jnp.stack([unit] * lax.psum(1, axis_name='row'), axis=0),...]
  transfers between devices with their start and end apart: 9 -> 11, of which waited for: 9 -> 11; matrix products, arithmetic and copies ran while one was open for 2% -> 2% of each run, Pallas kernels for 0% -> 0%
where the time goes in v1:
time: 1040 us
  waiting for transfers between devices  516 us (50%)
  blocking collectives  434 us (42%)
  local copies, waits for them, and re-layouts  39.2 us (4%)
  starting transfers between devices  17.8 us (2%)
  between operations  14.6 us (1%)
    psum x5, waiting for transfers between devices, settle(): summed = lax.psum(partial_value, 'col')  402 us
    psum x5, blocking collectives, settle(): summed = lax.psum(partial_value, 'col')  377 us
    all_gather x1, waiting for transfers between devices, per_device(): lax.all_gather(rhs_half[0, 1:3].astype(jnp.bfloat16), ('row', 'col'), axi...  70.4 us
    all_to_all x5, blocking collectives, settle(): lax.all_to_all(jnp.stack([unit] * lax.psum(1, axis_name='row'), axis=0),...  57.2 us
    all_to_all x4, waiting for transfers between devices, settle(): lax.all_to_all(jnp.stack([unit] * lax.psum(1, axis_name='row'), axis=0),...  22.3 us
    psum x1, waiting for transfers between devices, per_device(): root_terms = lax.psum(root_terms, 'gz')  21.4 us
  transfers between devices with their start and end apart: 11, of which 11 were waited for; matrix products, arithmetic and copies ran while one was open for 2% of the time, Pallas kernels for 0%

profile of v1, /device:TPU:0, one launch (start us, length us, event | category | flops | bytes accessed | tf_op | source)
XLA Modules:
  0.0 1041.0 jit_solution(16283220339171751882)
XLA Ops:
  8.9 70.4 %all-gather.3.cloned.1.call-done = bf16[1,2,64,4096]{2,1,0,3:T(2,128)(2,1)} async-done(((bf16[1,2,64,64]{2,1,0,3:T(2,128)(2,1)}), bf16[1,2,64,4096]{2,1,0,3:T(2,128)(2,1)}) %all-gather.3.cloned.1.call-update) | async-done | bytes 1048592 | tf_op jit(solution)/shard_map/all_gather | solution.py:65
  79.3 1.0 constant_dynamic-slice_fusion.6
  80.4 1.5 fusion.6
  83.3 83.1 %all-reduce.12.cloned.1.call-done = f32[2,64,1024]{2,1,0:T(8,128)} async-done(((f32[2,64,1024]{2,1,0:T(8,128)}), f32[2,64,1024]{2,1,0:T(8,128)}) %all-reduce.12.cloned.1.call-update) | async-done | bytes 524304 | tf_op jit(solution)/shard_map/psum | solution.py:28
  166.5 1.1 convert_element_type.70
  167.5 1.1 stack.18
  168.7 4.4 all-to-all-start
  174.0 1.1 slice.63
  175.1 2.3 slice.51
  177.4 9.0 all-to-all-done
  186.4 1.4 copy.43
  189.5 75.3 %all-reduce.23 = bf16[1,64,1024]{2,1,0:T(8,128)(2,1)} all-reduce(f32[1,64,1024]{2,1,0:T(8,128)S(1)} %dynamic_update_slice.31), channel_id=1, replica_groups=mesh['row'=4,'col'=16,'gz'=2] {'col'}, use_global_device_ids=true, to_apply=%region_1.0 | all-reduce | flops 65536 | bytes 393216 | tf_op jit(solution)/shard_map/psum | solution.py:28
  265.8 10.5 %all_to_all.45 = bf16[4,1,64,1024]{3,2,1,0:T(8,128)(2,1)S(1)} all-to-all(bf16[4,1,64,1024]{3,2,1,0:T(8,128)(2,1)S(1)} %stack.19), channel_id=1, replica_groups=mesh['row'=4,'col'=16,'gz'=2] {'row'}, dimensions={0} | all-to-all | bytes 1048576 | tf_op jit(solution)/shard_map/all_to_all | solution.py:32
  276.3 1.3 fusion.14
  278.8 80.0 %all-reduce.14.cloned.1.call-done = f32[1,64,1024]{2,1,0:T(8,128)} async-done(((f32[1,64,1024]{2,1,0:T(8,128)}), f32[1,64,1024]{2,1,0:T(8,128)}) %all-reduce.14.cloned.1.call-update) | async-done | bytes 262160 | tf_op jit(solution)/shard_map/psum | solution.py:28
  360.6 4.4 all-to-all-start.2
  365.1 1.3 slice.64
  366.3 2.5 slice.55
  368.9 4.3 all-to-all-done.2
  373.2 1.1 copy.45
  374.3 1.1 fusion.3
  375.5 21.4 %all-reduce.16.cloned.1.call-done = f32[1,64,1024]{2,1,0:T(8,128)} async-done(((f32[1,64,1024]{2,1,0:T(8,128)}), f32[1,64,1024]{2,1,0:T(8,128)}) %all-reduce.16.cloned.1.call-update) | async-done | bytes 262160 | tf_op jit(solution)/shard_map/psum | solution.py:79
  397.8 1.4 dynamic_update_slice.33
  399.2 77.5 %all-reduce.24 = bf16[1,64,1024]{2,1,0:T(8,128)(2,1)S(1)} all-reduce(f32[1,64,1024]{2,1,0:T(8,128)} %dynamic_update_slice.33), channel_id=1, replica_groups=mesh['row'=4,'col'=16,'gz'=2] {'col'}, use_global_device_ids=true, to_apply=%region_4.0 | all-reduce | flops 65536 | bytes 393216 | tf_op jit(solution)/shard_map/psum | solution.py:28
  476.8 12.3 %all_to_all.46 = bf16[4,1,64,1024]{3,2,1,0:T(8,128)(2,1)S(1)} all-to-all(bf16[4,1,64,1024]{3,2,1,0:T(8,128)(2,1)S(1)} %stack.21), channel_id=1, replica_groups=mesh['row'=4,'col'=16,'gz'=2] {'row'}, dimensions={0} | all-to-all | bytes 1048576 | tf_op jit(solution)/shard_map/all_to_all | solution.py:32
  489.8 71.8 %all-reduce.25 = bf16[1,64,1024]{2,1,0:T(8,128)(2,1)S(1)} all-reduce(f32[1,64,1024]{2,1,0:T(8,128)S(1)} %dynamic_update_slice.34), channel_id=1, replica_groups=mesh['row'=4,'col'=16,'gz'=2] {'col'}, use_global_device_ids=true, to_apply=%region_5.0 | all-reduce | flops 65536 | bytes 393216 | tf_op jit(solution)/shard_map/psum | solution.py:28
  561.7 10.5 %all_to_all.47 = bf16[4,1,64,1024]{3,2,1,0:T(8,128)(2,1)S(1)} all-to-all(bf16[4,1,64,1024]{3,2,1,0:T(8,128)(2,1)S(1)} %stack.22), channel_id=1, replica_groups=mesh['row'=4,'col'=16,'gz'=2] {'row'}, dimensions={0} | all-to-all | bytes 1048576 | tf_op jit(solution)/shard_map/all_to_all | solution.py:32
  572.3 1.4 fusion.28
  574.9 80.6 %all-reduce.18.cloned.1.call-done = f32[1,64,1024]{2,1,0:T(8,128)} async-done(((f32[1,64,1024]{2,1,0:T(8,128)}), f32[1,64,1024]{2,1,0:T(8,128)}) %all-reduce.18.cloned.1.call-update) | async-done | bytes 262160 | tf_op jit(solution)/shard_map/psum | solution.py:28
  657.4 4.4 all-to-all-start.5
  663.5 6.4 all-to-all-done.5
  670.0 1.1 copy.48
  671.1 1.4 convolution_negate_fusion
  673.8 74.5 %all-reduce.26 = bf16[1,64,1024]{2,1,0:T(8,128)(2,1)S(1)} all-reduce(f32[1,64,1024]{2,1,0:T(8,128)S(1)} %dynamic_update_slice.36), channel_id=1, replica_groups=mesh['row'=4,'col'=16,'gz'=2] {'col'}, use_global_device_ids=true, to_apply=%region_7.0 | all-reduce | flops 65536 | bytes 393216 | tf_op jit(solution)/shard_map/psum | solution.py:28
  748.4 10.5 %all_to_all.48 = bf16[4,1,64,1024]{3,2,1,0:T(8,128)(2,1)S(1)} all-to-all(bf16[4,1,64,1024]{3,2,1,0:T(8,128)(2,1)S(1)} %stack.24), channel_id=1, replica_groups=mesh['row'=4,'col'=16,'gz'=2] {'row'}, dimensions={0} | all-to-all | bytes 1048576 | tf_op jit(solution)/shard_map/all_to_all | solution.py:32
  758.9 1.3 fusion.12
  761.4 80.0 %all-reduce.20.cloned.1.call-done = f32[1,64,1024]{2,1,0:T(8,128)} async-done(((f32[1,64,1024]{2,1,0:T(8,128)}), f32[1,64,1024]{2,1,0:T(8,128)}) %all-reduce.20.cloned.1.call-update) | async-done | bytes 262160 | tf_op jit(solution)/shard_map/psum | solution.py:28
  843.2 4.4 all-to-all-start.7
  847.6 1.5 fusion.50
  849.1 1.5 slice.60
  850.6 1.5 slice.58
  852.2 1.1 fusion.24
  853.2 2.6 all-to-all-done.7
  855.8 1.1 copy.50
  858.6 77.8 %all-reduce.27 = bf16[2,64,1024]{2,1,0:T(8,128)(2,1)S(1)} all-reduce(f32[2,64,1024]{2,1,0:T(8,128)S(1)} %dynamic_update_slice.38), channel_id=1, replica_groups=mesh['row'=4,'col'=16,'gz'=2] {'col'}, use_global_device_ids=true, to_apply=%region_9.0 | all-reduce | flops 131072 | bytes 786432 | tf_op jit(solution)/shard_map/psum | solution.py:28
  936.6 13.4 %all_to_all.49 = bf16[4,2,64,1024]{3,2,1,0:T(8,128)(2,1)S(1)} all-to-all(bf16[4,2,64,1024]{3,2,1,0:T(8,128)(2,1)S(1)} %stack.26), channel_id=1, replica_groups=mesh['row'=4,'col'=16,'gz'=2] {'row'}, dimensions={0} | all-to-all | bytes 2097152 | tf_op jit(solution)/shard_map/all_to_all | solution.py:32
  951.8 1.5 dynamic-slice_bitcast_fusion
  954.1 78.5 %all-reduce.22.cloned.1.call-done = f32[2,64,1024]{2,1,0:T(8,128)} async-done(((f32[2,64,1024]{2,1,0:T(8,128)}), f32[2,64,1024]{2,1,0:T(8,128)}) %all-reduce.22.cloned.1.call-update) | async-done | bytes 524304 | tf_op jit(solution)/shard_map/psum | solution.py:28
  (96 shorter events, 26.7 us)
Async XLA Ops:
  7.2 481.9 %copy-start = (bf16[256,1024]{1,0:T(8,128)(2,1)S(1)}, bf16[256,1024]{1,0:T(8,128)(2,1)}, u32[]{:S(2)}) copy-start(bf16[256,1024]{1,0:T(8,128)(2,1)} %param.18) | copy-start | bytes 1572868
  7.2 72.2 %all-gather.3.cloned.1.call-start = ((), (), s32[]{:S(2)}) async-start(), calls=%async_computation.15 | async-start | bytes 2129920 | tf_op jit(solution)/shard_map/all_gather | solution.py:65
  8.9 157.6 %all-reduce.12.cloned.1.call-start = ((), (), s32[]{:S(2)}) async-start(), calls=%async_computation.9 | async-start | bytes 1048576 | tf_op jit(solution)/shard_map/psum | solution.py:28
  82.5 0.8 copy-start.4
  83.3 89.8 %copy-start.2 = (bf16[1,5,256,1024]{3,2,1,0:T(8,128)(2,1)S(1)}, bf16[1,5,256,1024]{3,2,1,0:T(8,128)(2,1)}, u32[]{:S(2)}) copy-start(bf16[1,5,256,1024]{3,2,1,0:T(8,128)(2,1)} %param.12) | copy-start | bytes 7864324
  168.7 17.7 %all-to-all-start = ((bf16[4,2,64,1024]{3,2,1,0:T(8,128)(2,1)}), bf16[4,2,64,1024]{3,2,1,0:T(8,128)(2,1)}, u32[]{:S(2)}, u32[]{:S(2)}) async-start(bf16[4,2,64,1024]{3,2,1,0:T(8,128)(2,1)} %stack.18), calls=%async_computation | async-start | bytes 2097152 | tf_op jit(solution)/shard_map/all_to_all | solution.py:32
  173.1 185.7 %all-reduce.14.cloned.1.call-start = ((), (), s32[]{:S(2)}) async-start(), calls=%async_computation.10 | async-start | bytes 524288 | tf_op jit(solution)/shard_map/psum | solution.py:28
  173.1 0.7 copy-start.12
  186.4 1.5 copy-start.1
  278.1 0.7 copy-start.7
  360.6 12.6 %all-to-all-start.2 = ((bf16[4,1,64,1024]{3,2,1,0:T(8,128)(2,1)}), bf16[4,1,64,1024]{3,2,1,0:T(8,128)(2,1)}, u32[]{:S(2)}, u32[]{:S(2)}) async-start(bf16[4,1,64,1024]{3,2,1,0:T(8,128)(2,1)} %stack.20), calls=%async_computation.2 | async-start | bytes 1048576 | tf_op jit(solution)/shard_map/all_to_all | solution.py:32
  365.1 31.9 %all-reduce.16.cloned.1.call-start = ((), (), s32[]{:S(2)}) async-start(), calls=%async_computation.11 | async-start | bytes 524288 | tf_op jit(solution)/shard_map/psum | solution.py:79
  368.9 28.0 %copy-start.11 = (f32[64,64]{1,0:T(8,128)S(1)}, f32[64,64]{1,0:T(8,128)}, u32[]{:S(2)}) copy-start(f32[64,64]{1,0:T(8,128)} %param.11) | copy-start | bytes 49156
  375.5 280.1 %all-reduce.18.cloned.1.call-start = ((), (), s32[]{:S(2)}) async-start(), calls=%async_computation.12 | async-start | bytes 524288 | tf_op jit(solution)/shard_map/psum | solution.py:28
  572.2 89.6 %copy-start.13 = (s32[1,5,2,8]{3,2,1,0:T(2,128)S(1)}, s32[1,5,2,8]{3,2,1,0:T(2,128)}, u32[]{:S(2)}) copy-start(s32[1,5,2,8]{3,2,1,0:T(2,128)} %param.15) | copy-start | bytes 964
  572.2 89.6 %copy-start.3 = (bf16[1,5,256,1024]{3,2,1,0:T(8,128)(2,1)S(1)}, bf16[1,5,256,1024]{3,2,1,0:T(8,128)(2,1)}, u32[]{:S(2)}) copy-start(bf16[1,5,256,1024]{3,2,1,0:T(8,128)(2,1)} %param.14) | copy-start | bytes 7864324
  574.2 0.7 copy-start.8
  657.4 12.6 %all-to-all-start.5 = ((bf16[4,1,64,1024]{3,2,1,0:T(8,128)(2,1)}), bf16[4,1,64,1024]{3,2,1,0:T(8,128)(2,1)}, u32[]{:S(2)}, u32[]{:S(2)}) async-start(bf16[4,1,64,1024]{3,2,1,0:T(8,128)(2,1)} %stack.23), calls=%async_computation.5 | async-start | bytes 1048576 | tf_op jit(solution)/shard_map/all_to_all | solution.py:32
  661.8 179.6 %all-reduce.20.cloned.1.call-start = ((), (), s32[]{:S(2)}) async-start(), calls=%async_computation.13 | async-start | bytes 524288 | tf_op jit(solution)/shard_map/psum | solution.py:28
  671.0 2.3 copy-start.10
  760.7 0.7 copy-start.9
  843.2 12.6 %all-to-all-start.7 = ((bf16[4,1,64,1024]{3,2,1,0:T(8,128)(2,1)}), bf16[4,1,64,1024]{3,2,1,0:T(8,128)(2,1)}, u32[]{:S(2)}, u32[]{:S(2)}) async-start(bf16[4,1,64,1024]{3,2,1,0:T(8,128)(2,1)} %stack.25), calls=%async_computation.7 | async-start | bytes 1048576 | tf_op jit(solution)/shard_map/all_to_all | solution.py:32
  847.6 185.0 %all-reduce.22.cloned.1.call-start = ((), (), s32[]{:S(2)}) async-start(), calls=%async_computation.14 | async-start | bytes 1048576 | tf_op jit(solution)/shard_map/psum | solution.py:28
  936.6 13.6 %copy-start.6 = (bf16[1,3,256,1024]{3,2,1,0:T(8,128)(2,1)S(1)}, bf16[1,3,256,1024]{3,2,1,0:T(8,128)(2,1)}, u32[]{:S(2)}) copy-start(bf16[1,3,256,1024]{3,2,1,0:T(8,128)(2,1)} %param.17) | copy-start | bytes 4718596
  951.0 0.8 copy-start.5
Sparse Core Ops, SparseCore 0:
  11.4 67.8 all-gather.2
  83.4 82.9 all-reduce.11
  278.9 79.8 all-reduce.13
  375.6 21.2 all-reduce.15
  575.0 80.4 all-reduce.17
  761.5 79.7 all-reduce.19
  952.0 80.5 all-reduce.21
